TPU v7x, 32 devices: a whole 2x2x4 slice. The times are simulated.
32 devices in a mesh: doc: 8 (over z, y), term: 4 (over x, core).
Axes of the slice: x: 2, y: 2, z: 4, core: 2. Of those that a mesh axis runs over, the one named last changes fastest.
Arguments:
- tfidf: bfloat16 [4096, 8192], P('term', 'doc'), may hold values from 50 to 1000
- pattern: int32 [32, 64], P('term', 'doc'), may hold values 0 or 1
- factor_w: bfloat16 [4096, 256], P('term'), may hold values from 0.29882812 to 3
- factor_h: bfloat16 [256, 8192], P(None, 'doc'), may hold values from 0.29882812 to 3
Outputs:
- updated_w: bfloat16 [4096, 256], P('term')
- updated_h: bfloat16 [256, 8192], P(None, 'doc')
All inputs are finite; a program needn't handle non-finite values. No bound on the sum of `pattern` on one device may be relied on, other than what follows from the above.
Results may differ from a plain program's by a relative error of at most 0.0004.
The roundings to bfloat16 on the way count: a program that leaves them out, or rounds other values in their place, can miss the bound.
Values may be sent and summed in bfloat16 or wider, within the bound.
No kernel may reach another device: no remote copies, remote signals or barrier semaphores. Data moves between devices by JAX's collectives and lax.ppermute only.
A program may use at most 64 MiB of HBM per device.

v0:
```python
import jax
import jax.numpy as jnp
from jax import lax
from jax.sharding import PartitionSpec as P

BLOCK = 128


def expand(pattern):
    block_rows, block_cols = pattern.shape
    spread = jnp.broadcast_to(pattern[:, None, :, None], (block_rows, BLOCK, block_cols, BLOCK))
    return spread.reshape(block_rows * BLOCK, block_cols * BLOCK)


def contract_first(operand_one, operand_two):
    return lax.dot_general(
        operand_one, operand_two, (((0,), (0,)), ((), ())), preferred_element_type=jnp.float32
    )


def contract_last(operand_one, operand_two):
    return lax.dot_general(
        operand_one, operand_two, (((1,), (1,)), ((), ())), preferred_element_type=jnp.float32
    )


def on_device(tfidf, pattern, factor_w, factor_h):
    masked = tfidf * expand(pattern).astype(jnp.bfloat16)
    gram_part = contract_first(factor_w, factor_w)
    numer_part = contract_first(factor_w, masked)
    gram_w = lax.psum(gram_part, "term")
    numerator = lax.psum_scatter(numer_part, "term", scatter_dimension=1, tiled=True)
    share_width = numerator.shape[1]
    old_share = lax.dynamic_slice_in_dim(
        factor_h, lax.axis_index("term") * share_width, share_width, 1
    )
    denominator = jnp.dot(
        gram_w.astype(jnp.bfloat16), old_share, preferred_element_type=jnp.float32
    )
    h_part = (old_share.astype(jnp.float32) * numerator / denominator).astype(jnp.bfloat16)
    new_h = lax.all_gather(h_part, "term", axis=1, tiled=True)
    gram_h_part = contract_last(new_h, new_h)
    term_topic, gram_h = lax.psum((contract_last(masked, new_h), gram_h_part), "doc")
    denominator = jnp.dot(factor_w, gram_h.astype(jnp.bfloat16), preferred_element_type=jnp.float32)
    new_w = (factor_w.astype(jnp.float32) * term_topic / denominator).astype(jnp.bfloat16)
    return (new_w, new_h)


def solution(mesh):
    placed = (P("term", "doc"), P("term", "doc"), P("term", None), P(None, "doc"))
    return jax.shard_map(
        on_device,
        mesh=mesh,
        in_specs=placed,
        out_specs=(P("term", None), P(None, "doc")),
        check_vma=False,
    )
```

profile of v0, /device:TPU:0, one launch (start us, length us, event | category | flops | bytes accessed | tf_op | source)
XLA Modules:
  0.0 143.6 jit_solution(14670027527547338195)
XLA Ops:
  7.2 0.0 copy-start
  7.2 0.0 copy-start.1
  7.2 0.0 reduce-scatter.2.cloned.1.call-start
  7.2 0.8 convert_element_type.26
  8.0 0.3 broadcast_in_dim.2
  8.4 0.0 copy-start.2
  8.4 1.3 copy-done.2
  9.7 0.0 copy-done.1
  9.7 3.5 %convolution_bitcast_fusion = f32[256,1024]{0,1:T(8,128)} fusion(bf16[1024,256]{1,0:T(8,128)(2,1)S(1)} %copy-done.1, bf16[1024,1024]{1,0:T(8,128)(2,1)} %param.4, bf16[128,8,8,128]{3,2,1,0:T(8,128)(2,1)S(1)} %bitcast.24), kind=kOutput, calls=%fused_computation.1 | convolution fusion | flops 537919488 | bytes 5767168 | tf_op jit(solution)/shard_map/dot_general | solution.py:16
  13.2 0.0 reduce-scatter.2.cloned.1.call-update
  13.3 0.0 all-reduce.4.cloned.1.call-start
  13.3 0.0 copy-done
  13.4 0.1 copy.12
  13.5 0.3 fusion.6
  13.8 16.3 %all-reduce.5 = bf16[256,256]{1,0:T(8,128)(2,1)S(1)} all-reduce(f32[256,256]{1,0:T(8,128)S(1)} %fusion.6), channel_id=1, replica_groups=mesh['doc'=8,'term'=4] {'term'}, use_global_device_ids=true, to_apply=%region_1.0 | all-reduce | flops 65536 | bytes 393216 | tf_op jit(solution)/shard_map/psum | solution.py:31
  30.1 10.8 %reduce-scatter.2.cloned.1.call-done = f32[256,256]{0,1:T(8,128)} async-done(((f32[256,1024]{0,1:T(8,128)}), f32[256,256]{0,1:T(8,128)}) %reduce-scatter.2.cloned.1.call-update) | async-done | bytes 262160 | tf_op jit(solution)/shard_map/reduce_scatter | solution.py:32
  40.9 1.2 fusion.2
  42.1 6.6 %all_gather.3 = bf16[256,1024]{0,1:T(8,128)(2,1)S(1)} all-gather(bf16[256,256]{0,1:T(8,128)(2,1)S(1)} %fusion.2), channel_id=1, replica_groups=mesh['doc'=8,'term'=4] {'term'}, dimensions={1}, use_global_device_ids=true | all-gather | bytes 655360 | tf_op jit(solution)/shard_map/all_gather | solution.py:41
  48.7 3.9 %fusion.3 = f32[1024,256]{1,0:T(8,128)} fusion(bf16[256,1024]{0,1:T(8,128)(2,1)S(1)} %all_gather.3, bf16[1024,1024]{1,0:T(8,128)(2,1)} %param.4, bf16[128,8,8,128]{3,2,1,0:T(8,128)(2,1)} %bitcast.25), kind=kOutput, calls=%fused_computation.7 | convolution fusion | flops 537919488 | bytes 5767168 | tf_op jit(solution)/shard_map/dot_general | solution.py:22
  52.6 0.0 all-reduce.4.cloned.1.call-update
  52.6 1.0 copy.9
  53.6 0.3 fusion.7
  54.0 41.6 %all-reduce.6 = bf16[256,256]{1,0:T(8,128)(2,1)S(1)} all-reduce(f32[256,256]{1,0:T(8,128)S(1)} %fusion.7), channel_id=1, replica_groups=mesh['doc'=8,'term'=4] {'doc'}, use_global_device_ids=true, to_apply=%region_3.0 | all-reduce | flops 65536 | bytes 393216 | tf_op jit(solution)/shard_map/psum | solution.py:43
  95.6 38.9 %all-reduce.4.cloned.1.call-done = f32[1024,256]{1,0:T(8,128)} async-done(((f32[1024,256]{1,0:T(8,128)}), f32[1024,256]{1,0:T(8,128)}) %all-reduce.4.cloned.1.call-update) | async-done | bytes 1048592 | tf_op jit(solution)/shard_map/psum | solution.py:43
  134.5 2.3 %fusion.1 = bf16[1024,256]{1,0:T(8,128)(2,1)} fusion(bf16[1024,256]{1,0:T(8,128)(2,1)S(1)} %copy-done.1, f32[1024,256]{1,0:T(8,128)} %all-reduce.4.cloned.1.call-done, bf16[256,256]{1,0:T(8,128)(2,1)S(1)} %all-reduce.6), kind=kOutput, calls=%fused_computation.4 | convolution fusion | flops 135266304 | bytes 2228224 | tf_op jit(solution)/shard_map/dot_general | solution.py:44
  (1 shorter events, 0.0 us)
Async XLA Ops:
  7.2 6.2 %copy-start = (bf16[256,1024]{1,0:T(8,128)(2,1)S(1)}, bf16[256,1024]{1,0:T(8,128)(2,1)}, u32[]{:S(2)}) copy-start(bf16[256,1024]{1,0:T(8,128)(2,1)} %param.7) | copy-start | bytes 1572868
  7.2 2.5 %copy-start.1 = (bf16[1024,256]{1,0:T(8,128)(2,1)S(1)}, bf16[1024,256]{1,0:T(8,128)(2,1)}, u32[]{:S(2)}) copy-start(bf16[1024,256]{1,0:T(8,128)(2,1)} %param.6) | copy-start | bytes 1572868
  7.2 33.7 %reduce-scatter.2.cloned.1.call-start = ((), (), s32[]{:S(2)}) async-start(), calls=%async_computation.1 | async-start | bytes 1310720 | tf_op jit(solution)/shard_map/reduce_scatter | solution.py:32
  8.4 1.4 copy-start.2
  13.3 121.2 %all-reduce.4.cloned.1.call-start = ((), (), s32[]{:S(2)}) async-start(), calls=%async_computation.2 | async-start | bytes 2097152 | tf_op jit(solution)/shard_map/psum | solution.py:43
Sparse Core Ops, SparseCore 0:
  13.4 27.4 reduce-scatter.1
  52.8 81.6 all-reduce.3
where the time goes:
time: 144 us
  blocking collectives  64.4 us (45%)
  waiting for transfers between devices  49.8 us (35%)
  between operations  14.1 us (10%)
  matrix products  11.6 us (8%)
  local copies, waits for them, and re-layouts  2.82 us (2%)
    psum x1, blocking collectives, on_device(): lax.psum((contract_last(masked, new_h), gram_h_part), 'doc')  41.6 us
    psum x1, waiting for transfers between devices, on_device(): lax.psum((contract_last(masked, new_h), gram_h_part), 'doc')  38.9 us
    psum x1, blocking collectives, on_device(): gram_w = lax.psum(gram_part, 'term')  16.3 us
    reduce_scatter x1, waiting for transfers between devices, on_device(): lax.psum_scatter(numer_part, 'term', scatter_dimension=1, tiled=True)  10.8 us
    all_gather x1, blocking collectives, on_device(): new_h = lax.all_gather(h_part, 'term', axis=1, tiled=True)  6.58 us
    dot_general x2, matrix products, contract_last(): lax.dot_general(operand_one, operand_two, (((1,), (1,)), ((), ())), prefe...  4.26 us
    dot_general x2, matrix products, contract_first(): lax.dot_general(operand_one, operand_two, (((0,), (0,)), ((), ())), prefe...  3.86 us
  transfers between devices with their start and end apart: 2, of which 2 were waited for; matrix products, arithmetic and copies ran while one was open for 1% of the time, Pallas kernels for 0%

commit v1 on v0

--- a/solution.py
+++ b/solution.py
@@ -28,7 +28,7 @@
     masked = tfidf * expand(pattern).astype(jnp.bfloat16)
     gram_part = contract_first(factor_w, factor_w)
     numer_part = contract_first(factor_w, masked)
-    gram_w = lax.psum(gram_part, "term")
+    gram_w = jnp.sum(lax.all_gather(gram_part, "term"), axis=0)
     numerator = lax.psum_scatter(numer_part, "term", scatter_dimension=1, tiled=True)
     share_width = numerator.shape[1]
     old_share = lax.dynamic_slice_in_dim(

time: 144 us -> 160 us (1.11)
  waiting for transfers between devices: 49.8 us -> 80.3 us
  blocking collectives: 64.4 us -> 48.2 us
    psum x1 -> x0, blocking collectives: 16.3 us -> none  [on_device(): gram_w = lax.psum(gram_part, 'term')]
    all_gather x0 -> x1, waiting for transfers between devices: none -> 15.3 us  [on_device(): gram_w = jnp.sum(lax.all_gather(gram_part, 'term'), axis=0)]
    reduce_scatter x1, waiting for transfers between devices: 10.8 us -> 26 us  [on_device(): lax.psum_scatter(numer_part, 'term', scatter_dimension=1, tiled=True)]
  transfers between devices with their start and end apart: 2 -> 3, of which waited for: 2 -> 3; matrix products, arithmetic and copies ran while one was open for 1% -> 4% of each run, Pallas kernels for 0% -> 0%
where the time goes in v1:
time: 160 us; the launch traced here: 159 us
  waiting for transfers between devices  80.3 us (50%)
  blocking collectives  48.2 us (30%)
  between operations  13.8 us (9%)
  matrix products  12.1 us (8%)
  local copies, waits for them, and re-layouts  2.82 us (2%)
  other arithmetic  1.99 us (1%)
    psum x1, blocking collectives, on_device(): lax.psum((contract_last(masked, new_h), gram_h_part), 'doc')  41.6 us
    psum x1, waiting for transfers between devices, on_device(): lax.psum((contract_last(masked, new_h), gram_h_part), 'doc')  38.9 us
    reduce_scatter x1, waiting for transfers between devices, on_device(): lax.psum_scatter(numer_part, 'term', scatter_dimension=1, tiled=True)  26 us
    all_gather x1, waiting for transfers between devices, on_device(): gram_w = jnp.sum(lax.all_gather(gram_part, 'term'), axis=0)  15.3 us
    all_gather x1, blocking collectives, on_device(): new_h = lax.all_gather(h_part, 'term', axis=1, tiled=True)  6.6 us
    dot_general x2, matrix products, contract_first(): lax.dot_general(operand_one, operand_two, (((0,), (0,)), ((), ())), prefe...  4.33 us
    dot_general x2, matrix products, contract_last(): lax.dot_general(operand_one, operand_two, (((1,), (1,)), ((), ())), prefe...  4.26 us
  transfers between devices with their start and end apart: 3, of which 3 were waited for; matrix products, arithmetic and copies ran while one was open for 4% of the time, Pallas kernels for 0%

profile of v1, /device:TPU:0, one launch (start us, length us, event | category | flops | bytes accessed | tf_op | source)
XLA Modules:
  0.0 159.4 jit_solution(15695729897140126332)
XLA Ops:
  7.2 0.0 copy-start
  7.2 0.0 copy-start.1
  7.2 0.0 copy-start.3
  7.2 0.0 all-gather.3.cloned.1.call-start
  7.2 2.4 %fusion.6 = f32[256,256]{1,0:T(8,128)} fusion(bf16[1024,256]{1,0:T(8,128)(2,1)} %param.6), kind=kOutput, calls=%fused_computation.11 | convolution fusion | flops 134217728 | bytes 786432 | tf_op jit(solution)/shard_map/dot_general | solution.py:16
  9.6 0.0 all-gather.3.cloned.1.call-update
  9.7 0.0 reduce-scatter.2.cloned.1.call-start
  9.7 0.7 convert_element_type.26
  10.4 0.3 broadcast_in_dim.2
  10.7 0.0 copy-start.2
  10.8 1.3 copy-done.2
  12.1 0.0 copy-done.1
  12.1 0.0 copy-done.3
  12.1 1.9 %convolution_bitcast_fusion = f32[256,1024]{0,1:T(8,128)} fusion(bf16[1024,256]{1,0:T(8,128)(2,1)S(1)} %copy-done.1, bf16[1024,1024]{1,0:T(8,128)(2,1)S(1)} %copy-done.3, bf16[128,8,8,128]{3,2,1,0:T(8,128)(2,1)S(1)} %bitcast.25), kind=kOutput, calls=%fused_computation.1 | convolution fusion | flops 537919488 | bytes 5767168 | tf_op jit(solution)/shard_map/dot_general | solution.py:16
  14.0 0.0 reduce-scatter.2.cloned.1.call-update
  14.1 0.0 all-reduce.3.cloned.1.call-start
  14.1 0.0 copy-done
  14.2 0.1 copy.12
  14.3 15.3 %all-gather.3.cloned.1.call-done = f32[1024,256]{1,0:T(8,128)} async-done(((f32[256,256]{1,0:T(8,128)}), f32[1024,256]{1,0:T(8,128)}) %all-gather.3.cloned.1.call-update) | async-done | bytes 1048592 | tf_op jit(solution)/shard_map/all_gather | solution.py:31
  29.6 1.3 reduce_sum.9
  30.9 26.0 %reduce-scatter.2.cloned.1.call-done = f32[256,256]{0,1:T(8,128)} async-done(((f32[256,1024]{0,1:T(8,128)}), f32[256,256]{0,1:T(8,128)}) %reduce-scatter.2.cloned.1.call-update) | async-done | bytes 262160 | tf_op jit(solution)/shard_map/reduce_scatter | solution.py:32
  56.9 1.2 fusion.2
  58.1 6.6 %all_gather.11 = bf16[256,1024]{0,1:T(8,128)(2,1)S(1)} all-gather(bf16[256,256]{0,1:T(8,128)(2,1)S(1)} %fusion.2), channel_id=1, replica_groups=mesh['doc'=8,'term'=4] {'term'}, dimensions={1}, use_global_device_ids=true | all-gather | bytes 655360 | tf_op jit(solution)/shard_map/all_gather | solution.py:41
  64.7 3.9 %fusion.3 = f32[1024,256]{1,0:T(8,128)} fusion(bf16[256,1024]{0,1:T(8,128)(2,1)S(1)} %all_gather.11, bf16[1024,1024]{1,0:T(8,128)(2,1)} %param.4, bf16[128,8,8,128]{3,2,1,0:T(8,128)(2,1)} %bitcast.26), kind=kOutput, calls=%fused_computation.7 | convolution fusion | flops 537919488 | bytes 5767168 | tf_op jit(solution)/shard_map/dot_general | solution.py:22
  68.7 0.0 all-reduce.3.cloned.1.call-update
  68.7 1.0 copy.9
  69.7 0.3 fusion.7
  70.0 41.6 %all-reduce.4 = bf16[256,256]{1,0:T(8,128)(2,1)S(1)} all-reduce(f32[256,256]{1,0:T(8,128)S(1)} %fusion.7), channel_id=1, replica_groups=mesh['doc'=8,'term'=4] {'doc'}, use_global_device_ids=true, to_apply=%region_3.0 | all-reduce | flops 65536 | bytes 393216 | tf_op jit(solution)/shard_map/psum | solution.py:43
  111.6 38.9 %all-reduce.3.cloned.1.call-done = f32[1024,256]{1,0:T(8,128)} async-done(((f32[1024,256]{1,0:T(8,128)}), f32[1024,256]{1,0:T(8,128)}) %all-reduce.3.cloned.1.call-update) | async-done | bytes 1048592 | tf_op jit(solution)/shard_map/psum | solution.py:43
  150.5 2.3 %fusion.1 = bf16[1024,256]{1,0:T(8,128)(2,1)} fusion(bf16[1024,256]{1,0:T(8,128)(2,1)S(1)} %copy-done.1, f32[1024,256]{1,0:T(8,128)} %all-reduce.3.cloned.1.call-done, bf16[256,256]{1,0:T(8,128)(2,1)S(1)} %all-reduce.4), kind=kOutput, calls=%fused_computation.4 | convolution fusion | flops 135266304 | bytes 2228224 | tf_op jit(solution)/shard_map/dot_general | solution.py:44
  (1 shorter events, 0.0 us)
Async XLA Ops:
  7.2 7.0 %copy-start = (bf16[256,1024]{1,0:T(8,128)(2,1)S(1)}, bf16[256,1024]{1,0:T(8,128)(2,1)}, u32[]{:S(2)}) copy-start(bf16[256,1024]{1,0:T(8,128)(2,1)} %param.7) | copy-start | bytes 1572868
  7.2 4.9 %copy-start.1 = (bf16[1024,256]{1,0:T(8,128)(2,1)S(1)}, bf16[1024,256]{1,0:T(8,128)(2,1)}, u32[]{:S(2)}) copy-start(bf16[1024,256]{1,0:T(8,128)(2,1)} %param.6) | copy-start | bytes 1572868
  7.2 4.9 %copy-start.3 = (bf16[1024,1024]{1,0:T(8,128)(2,1)S(1)}, bf16[1024,1024]{1,0:T(8,128)(2,1)}, u32[]{:S(2)}) copy-start(bf16[1024,1024]{1,0:T(8,128)(2,1)} %param.4) | copy-start | bytes 6291460
  7.2 22.4 %all-gather.3.cloned.1.call-start = ((), (), s32[]{:S(2)}) async-start(), calls=%async_computation.3 | async-start | bytes 1310720 | tf_op jit(solution)/shard_map/all_gather | solution.py:31
  9.7 47.3 %reduce-scatter.2.cloned.1.call-start = ((), (), s32[]{:S(2)}) async-start(), calls=%async_computation.1 | async-start | bytes 1310720 | tf_op jit(solution)/shard_map/reduce_scatter | solution.py:32
  10.7 1.3 copy-start.2
  14.1 136.5 %all-reduce.3.cloned.1.call-start = ((), (), s32[]{:S(2)}) async-start(), calls=%async_computation.2 | async-start | bytes 2097152 | tf_op jit(solution)/shard_map/psum | solution.py:43
Sparse Core Ops, SparseCore 0:
  10.1 19.4 all-gather.2
  32.1 24.7 reduce-scatter.1
  68.8 81.6 all-reduce.2
